TPU v7x, 256 devices: a whole 4x4x8 slice. The times are simulated.
256 devices in a mesh: row: 64 (over y, x_hi, z), col: 4 (over x_lo, core).
Axes of the slice: x: 4 (x_hi: 2, x_lo: 2; x = x_hi * 2 + x_lo), y: 4, z: 8, core: 2. Of those that a mesh axis runs over, the one named last changes fastest.
Arguments:
- operator: bfloat16 [32768, 32768], P('row', 'col'), may hold values from -0.0068359375 to 0.0068359375
- rhs: float32 [32, 32768], P(None, 'row'), may hold values from -72 to 72
- bodies: int32 [32768], P('row'), may hold values from 0 to 63, as said below
- weights: float32 [32768], P('row'), may hold values from 0.5 to 1.5
Outputs:
- basis: float32 [128, 32768], P(None, ('row', 'col'))
- hess: float32 [128, 96], replicated
- start_factor: float32 [32, 32], replicated
Inputs may be any that keep to these rules, and one draw needn't show every extreme that they name: Every one of the 64 bodies has at least one node.
All inputs are finite; a program needn't handle non-finite values.
Results may differ from a plain program's by a relative error of at most 0.0025.
Values may be sent and summed in bfloat16 or wider, within the bound.
A program may use at most 64 MiB of HBM per device.

v0:
```python
import jax
import jax.numpy as jnp
from jax import lax
from jax.sharding import Mesh
from jax.sharding import PartitionSpec as P

N = 32768
S = 32
BODIES = 64
STEPS = 3
COL = ("col_0", "col_1")
ROW_COL = ("row_0", "row_1", "row_2", "col_0", "col_1")
ROW = ("row_0", "row_1", "row_2")


def one_axis_at_a_time(shard, axes):
    for axis in axes:
        shard = lax.psum(shard, axis)
    return shard


def joined_along(parts, dim):
    parts = jnp.moveaxis(parts, 0, dim)
    lengths = parts.shape
    return parts.reshape(*lengths[:dim], lengths[dim] * lengths[dim + 1], *lengths[dim + 2 :])


def all_blocks(shard, axes, sequence):
    parts = shard
    for k in sequence:
        parts = lax.all_gather(parts, axes[k])
    done = sequence[::-1]
    back = [done.index(k) for k in range(len(axes))]
    parts = parts.transpose(*back, *range(len(axes), parts.ndim))
    return parts.reshape(-1, *shard.shape)


def whole_of(shard, axes, sequence, dim):
    return joined_along(all_blocks(shard, axes, sequence), dim)


def sent_to_all(shard, axis):
    copies = jnp.broadcast_to(shard, (lax.axis_size(axis), *shard.shape))
    return lax.all_to_all(copies, axis, split_axis=0, concat_axis=0, tiled=True)


def over_copies(shard, axis):
    everything = sent_to_all(shard, axis)
    return jnp.sum(everything, axis=0)


def product_t(left, right):
    return lax.dot_general(
        left,
        right,
        (((1,), (1,)), ((), ())),
        precision=lax.Precision.HIGHEST,
        preferred_element_type=jnp.float32,
    )


def local(operator, rhs, bodies, weights):
    col_index = lax.axis_index(COL)
    col_count = lax.axis_size(COL)
    row_width = rhs.shape[1]
    quarter = row_width // col_count

    def portion(values):
        return lax.dynamic_slice_in_dim(values, col_index * quarter, quarter, 1)

    onehot = (bodies[:, None] == jnp.arange(BODIES, dtype=jnp.int32)[None, :]).astype(jnp.float32)
    onehot_part = jnp.transpose(portion(onehot.T))
    gram_start = one_axis_at_a_time(product_t(portion(rhs), portion(rhs)), ROW_COL) / N
    start_low = jnp.linalg.cholesky(gram_start)
    basis_list = [lax.linalg.triangular_solve(start_low, rhs, left_side=True, lower=True)]
    col_width = operator.shape[1]
    columns = []
    for step_index in range(STEPS):
        current = basis_list[-1]
        current_low = current.astype(jnp.bfloat16)
        gathered = whole_of(current_low, ROW, (1, 2, 0), 1)
        col_block = lax.dynamic_slice_in_dim(gathered, col_index * col_width, col_width, 1)
        partial_terms = lax.dot_general(
            col_block, operator, (((1,), (1,)), ((), ())), preferred_element_type=jnp.float32
        )
        coupled = over_copies(partial_terms, COL)
        scaled = current_low.astype(jnp.float32) * weights[None, :]
        body_partial = jnp.dot(portion(scaled), onehot_part, precision=lax.Precision.HIGHEST)
        body_means = one_axis_at_a_time(body_partial, ROW_COL) * (BODIES / N)
        completion = weights[None, :] * product_t(body_means, onehot)
        image_block = 0.5 * current + coupled + completion
        stacked = jnp.concatenate(basis_list, axis=0)
        stacked_part = portion(stacked)
        image_part = portion(image_block)
        coef_raw, gram_raw = (
            one_axis_at_a_time(product_t(stacked_part, image_part), ROW_COL),
            one_axis_at_a_time(product_t(image_part, image_part), ROW_COL),
        )
        first_coef = coef_raw / N
        residual_one = image_block - jnp.dot(first_coef.T, stacked, precision=lax.Precision.HIGHEST)
        gram_block = gram_raw / N - jnp.dot(
            first_coef.T, first_coef, precision=lax.Precision.HIGHEST
        )
        factor_low = jnp.linalg.cholesky(gram_block)
        basis_list.append(
            lax.linalg.triangular_solve(factor_low, residual_one, left_side=True, lower=True)
        )
        pieces = [first_coef, factor_low.T]
        below = (STEPS - 1 - step_index) * S
        if below > 0:
            pieces.append(jnp.zeros((below, S), jnp.float32))
        columns.append(jnp.concatenate(pieces, axis=0))
    basis = portion(jnp.concatenate(basis_list, axis=0))
    return (basis, jnp.concatenate(columns, axis=1), start_low)


def solution(mesh):
    split = Mesh(mesh.devices.reshape(4, 2, 8, 2, 2), ("row_0", "row_1", "row_2", "col_0", "col_1"))
    placed = (P(ROW, COL), P(None, ROW), P(ROW), P(ROW))
    return jax.shard_map(
        local, mesh=split, in_specs=placed, out_specs=(P(None, ROW_COL), P(), P()), check_vma=False
    )
```

profile of v0, /device:TPU:1, one launch (start us, length us, event | category | flops | bytes accessed | tf_op | source)
XLA Modules:
  0.0 710.6 jit_solution(9784179976770746269)
XLA Ops:
  8.2 14.2 %psum.350 = f32[32,32]{0,1:T(8,128)S(1)} all-reduce(f32[32,32]{0,1:T(8,128)S(1)} %fusion.50), channel_id=1, replica_groups=mesh['row_0'=4,'row_1'=2,'row_2'=8,'col_0'=2,'col_1'=2] {'row_0'}, use_global_device_ids=true, to_apply=%region_0.0 | all-reduce | flops 1024 | bytes 8192 | tf_op jit(solution)/shard_map/psum | solution.py:18
  31.5 25.5 %psum.352 = f32[32,32]{0,1:T(8,128)S(1)} all-reduce(f32[32,32]{0,1:T(8,128)S(1)} %psum.351), channel_id=1, replica_groups=mesh['row_0'=4,'row_1'=2,'row_2'=8,'col_0'=2,'col_1'=2] {'row_2'}, use_global_device_ids=true, to_apply=%region_2.0 | all-reduce | flops 1024 | bytes 8192 | tf_op jit(solution)/shard_map/psum | solution.py:18
  62.2 18.9 %psum.354 = f32[32,32]{0,1:T(8,128)S(1)} all-reduce(f32[32,32]{0,1:T(8,128)S(1)} %psum.353), channel_id=1, replica_groups=mesh['row_0'=4,'row_1'=2,'row_2'=8,'col_0'=2,'col_1'=2] {'col_1'}, use_global_device_ids=true, to_apply=%region_4.0 | all-reduce | flops 1024 | bytes 8192 | tf_op jit(solution)/shard_map/psum | solution.py:18
  93.7 21.4 %all-gather.1 = bf16[16,32,512]{2,1,0:T(8,128)(2,1)} all-gather(bf16[2,32,512]{2,1,0:T(8,128)(2,1)S(1)} %bitcast.98), channel_id=3, replica_groups=mesh['row_0'=4,'row_1'=2,'row_2'=8,'col_0'=2,'col_1'=2] {'row_2'}, dimensions={0}, use_global_device_ids=true | all-gather | bytes 589824 | tf_op jit(solution)/shard_map/all_gather | solution.py:31
  116.8 33.1 %all-gather.13.cloned.1.call-done = bf16[32,2,32,512]{3,2,1,0:T(8,128)(2,1)} async-done(((bf16[8,2,32,512]{3,2,1,0:T(8,128)(2,1)}), bf16[32,2,32,512]{3,2,1,0:T(8,128)(2,1)}) %all-gather.13.cloned.1.call-update) | async-done | bytes 2097168 | tf_op jit(solution)/shard_map/all_gather | solution.py:31
  161.6 11.2 %psum.355 = f32[32,64]{1,0:T(8,128)S(1)} all-reduce(f32[32,64]{1,0:T(8,128)S(1)} %fusion.24), channel_id=1, replica_groups=mesh['row_0'=4,'row_1'=2,'row_2'=8,'col_0'=2,'col_1'=2] {'row_0'}, use_global_device_ids=true, to_apply=%region_8.11 | all-reduce | flops 2048 | bytes 16384 | tf_op jit(solution)/shard_map/psum | solution.py:18
  181.9 23.3 %psum.357 = f32[32,64]{1,0:T(8,128)S(1)} all-reduce(f32[32,64]{1,0:T(8,128)S(1)} %psum.356), channel_id=1, replica_groups=mesh['row_0'=4,'row_1'=2,'row_2'=8,'col_0'=2,'col_1'=2] {'row_2'}, use_global_device_ids=true, to_apply=%region_10.13 | all-reduce | flops 2048 | bytes 16384 | tf_op jit(solution)/shard_map/psum | solution.py:18
  211.0 18.1 %psum.359 = f32[32,64]{1,0:T(8,128)S(1)} all-reduce(f32[32,64]{1,0:T(8,128)S(1)} %psum.358), channel_id=1, replica_groups=mesh['row_0'=4,'row_1'=2,'row_2'=8,'col_0'=2,'col_1'=2] {'col_1'}, use_global_device_ids=true, to_apply=%region_12.15 | all-reduce | flops 2048 | bytes 16384 | tf_op jit(solution)/shard_map/psum | solution.py:18
  229.9 11.3 %all-reduce.5 = (f32[32,32]{0,1:T(8,128)S(1)}, f32[32,32]{0,1:T(8,128)S(1)}) all-reduce(f32[32,32]{0,1:T(8,128)S(1)} %fusion.45, f32[32,32]{0,1:T(8,128)S(1)} %fusion.59), channel_id=1, replica_groups=mesh['row_0'=4,'row_1'=2,'row_2'=8,'col_0'=2,'col_1'=2] {'row_0'}, use_global_device_ids=true, to_apply=%region_18.21 | all-reduce | flops 2048 | bytes 16384 | tf_op jit(solution)/shard_map/psum | solution.py:18
  249.3 20.2 %all-reduce.2 = (f32[32,32]{0,1:T(8,128)S(1)}, f32[32,32]{0,1:T(8,128)S(1)}) all-reduce(f32[32,32]{0,1:T(8,128)S(1)} %get-tuple-element.33, f32[32,32]{0,1:T(8,128)S(1)} %get-tuple-element.34), channel_id=1, replica_groups=mesh['row_0'=4,'row_1'=2,'row_2'=8,'col_0'=2,'col_1'=2] {'row_2'}, use_global_device_ids=true, to_apply=%region_20.23 | all-reduce | flops 2048 | bytes 16384 | tf_op jit(solution)/shard_map/psum | solution.py:18
  274.9 17.4 %all-reduce.8 = (f32[32,32]{0,1:T(8,128)S(1)}, f32[32,32]{0,1:T(8,128)S(1)}) all-reduce(f32[32,32]{0,1:T(8,128)S(1)} %get-tuple-element.27, f32[32,32]{0,1:T(8,128)S(1)} %get-tuple-element.28), channel_id=1, replica_groups=mesh['row_0'=4,'row_1'=2,'row_2'=8,'col_0'=2,'col_1'=2] {'col_1'}, use_global_device_ids=true, to_apply=%region_22.25 | all-reduce | flops 2048 | bytes 16384 | tf_op jit(solution)/shard_map/psum | solution.py:18
  304.7 21.7 %all-gather.4 = bf16[16,32,512]{2,1,0:T(8,128)(2,1)} all-gather(bf16[2,32,512]{2,1,0:T(8,128)(2,1)S(1)} %bitcast.99), channel_id=6, replica_groups=mesh['row_0'=4,'row_1'=2,'row_2'=8,'col_0'=2,'col_1'=2] {'row_2'}, dimensions={0}, use_global_device_ids=true | all-gather | bytes 589824 | tf_op jit(solution)/shard_map/all_gather | solution.py:31
  326.5 36.9 %all-gather.15.cloned.1.call-done = bf16[32,2,32,512]{3,2,1,0:T(8,128)(2,1)} async-done(((bf16[8,2,32,512]{3,2,1,0:T(8,128)(2,1)}), bf16[32,2,32,512]{3,2,1,0:T(8,128)(2,1)}) %all-gather.15.cloned.1.call-update) | async-done | bytes 2097168 | tf_op jit(solution)/shard_map/all_gather | solution.py:31
  396.8 23.3 %psum.372 = f32[32,64]{1,0:T(8,128)S(1)} all-reduce(f32[32,64]{1,0:T(8,128)S(1)} %psum.371), channel_id=1, replica_groups=mesh['row_0'=4,'row_1'=2,'row_2'=8,'col_0'=2,'col_1'=2] {'row_2'}, use_global_device_ids=true, to_apply=%region_26.29 | all-reduce | flops 2048 | bytes 16384 | tf_op jit(solution)/shard_map/psum | solution.py:18
  425.9 18.1 %psum.374 = f32[32,64]{1,0:T(8,128)S(1)} all-reduce(f32[32,64]{1,0:T(8,128)S(1)} %psum.373), channel_id=1, replica_groups=mesh['row_0'=4,'row_1'=2,'row_2'=8,'col_0'=2,'col_1'=2] {'col_1'}, use_global_device_ids=true, to_apply=%region_28.31 | all-reduce | flops 2048 | bytes 16384 | tf_op jit(solution)/shard_map/psum | solution.py:18
  444.7 11.3 %all-reduce.4 = (f32[64,32]{0,1:T(8,128)S(1)}, f32[32,32]{0,1:T(8,128)S(1)}) all-reduce(f32[64,32]{0,1:T(8,128)S(1)} %fusion.18, f32[32,32]{0,1:T(8,128)S(1)} %fusion.56), channel_id=1, replica_groups=mesh['row_0'=4,'row_1'=2,'row_2'=8,'col_0'=2,'col_1'=2] {'row_0'}, use_global_device_ids=true, to_apply=%region_34.37 | all-reduce | flops 3072 | bytes 24576 | tf_op jit(solution)/shard_map/psum | solution.py:18
  464.2 20.2 %all-reduce.1 = (f32[64,32]{0,1:T(8,128)S(1)}, f32[32,32]{0,1:T(8,128)S(1)}) all-reduce(f32[64,32]{0,1:T(8,128)S(1)} %get-tuple-element.31, f32[32,32]{0,1:T(8,128)S(1)} %get-tuple-element.32), channel_id=1, replica_groups=mesh['row_0'=4,'row_1'=2,'row_2'=8,'col_0'=2,'col_1'=2] {'row_2'}, use_global_device_ids=true, to_apply=%region_36.39 | all-reduce | flops 3072 | bytes 24576 | tf_op jit(solution)/shard_map/psum | solution.py:18
  489.8 17.4 %all-reduce.7 = (f32[64,32]{0,1:T(8,128)S(1)}, f32[32,32]{0,1:T(8,128)S(1)}) all-reduce(f32[64,32]{0,1:T(8,128)S(1)} %get-tuple-element.25, f32[32,32]{0,1:T(8,128)S(1)} %get-tuple-element.26), channel_id=1, replica_groups=mesh['row_0'=4,'row_1'=2,'row_2'=8,'col_0'=2,'col_1'=2] {'col_1'}, use_global_device_ids=true, to_apply=%region_38.41 | all-reduce | flops 3072 | bytes 24576 | tf_op jit(solution)/shard_map/psum | solution.py:18
  519.6 21.7 %all-gather.7 = bf16[16,32,512]{2,1,0:T(8,128)(2,1)} all-gather(bf16[2,32,512]{2,1,0:T(8,128)(2,1)S(1)} %bitcast.100), channel_id=9, replica_groups=mesh['row_0'=4,'row_1'=2,'row_2'=8,'col_0'=2,'col_1'=2] {'row_2'}, dimensions={0}, use_global_device_ids=true | all-gather | bytes 589824 | tf_op jit(solution)/shard_map/all_gather | solution.py:31
  541.5 11.8 %psum.385 = f32[32,64]{1,0:T(8,128)S(1)} all-reduce(f32[32,64]{1,0:T(8,128)S(1)} %fusion.20), channel_id=1, replica_groups=mesh['row_0'=4,'row_1'=2,'row_2'=8,'col_0'=2,'col_1'=2] {'row_0'}, use_global_device_ids=true, to_apply=%region_40.43 | all-reduce | flops 2048 | bytes 16384 | tf_op jit(solution)/shard_map/psum | solution.py:18
  562.5 22.1 %psum.387 = f32[32,64]{1,0:T(8,128)S(1)} all-reduce(f32[32,64]{1,0:T(8,128)S(1)} %psum.386), channel_id=1, replica_groups=mesh['row_0'=4,'row_1'=2,'row_2'=8,'col_0'=2,'col_1'=2] {'row_2'}, use_global_device_ids=true, to_apply=%region_42.45 | all-reduce | flops 2048 | bytes 16384 | tf_op jit(solution)/shard_map/psum | solution.py:18
  589.5 23.1 %psum.389 = f32[32,64]{1,0:T(8,128)S(1)} all-reduce(f32[32,64]{1,0:T(8,128)S(1)} %psum.388), channel_id=1, replica_groups=mesh['row_0'=4,'row_1'=2,'row_2'=8,'col_0'=2,'col_1'=2] {'col_1'}, use_global_device_ids=true, to_apply=%region_44.47 | all-reduce | flops 2048 | bytes 16384 | tf_op jit(solution)/shard_map/psum | solution.py:18
  651.1 20.3 %all-reduce = (f32[96,32]{0,1:T(8,128)S(1)}, f32[32,32]{0,1:T(8,128)S(1)}) all-reduce(f32[96,32]{0,1:T(8,128)S(1)} %get-tuple-element.29, f32[32,32]{0,1:T(8,128)S(1)} %get-tuple-element.30), channel_id=1, replica_groups=mesh['row_0'=4,'row_1'=2,'row_2'=8,'col_0'=2,'col_1'=2] {'row_2'}, use_global_device_ids=true, to_apply=%region_52.55 | all-reduce | flops 4096 | bytes 32768 | tf_op jit(solution)/shard_map/psum | solution.py:18
  676.5 18.7 %all-reduce.6 = (f32[96,32]{0,1:T(8,128)S(1)}, f32[32,32]{0,1:T(8,128)S(1)}) all-reduce(f32[96,32]{0,1:T(8,128)S(1)} %get-tuple-element.23, f32[32,32]{0,1:T(8,128)S(1)} %get-tuple-element.24), channel_id=1, replica_groups=mesh['row_0'=4,'row_1'=2,'row_2'=8,'col_0'=2,'col_1'=2] {'col_1'}, use_global_device_ids=true, to_apply=%region_54.57 | all-reduce | flops 4096 | bytes 32768 | tf_op jit(solution)/shard_map/psum | solution.py:18
  (117 shorter events, 215.1 us)
Async XLA Ops:
  7.2 0.8 copy-start
  7.2 142.7 %all-gather.13.cloned.1.call-start = ((), (), s32[]{:S(2)}) async-start(), calls=%async_computation.3 | async-start | bytes 2621440 | tf_op jit(solution)/shard_map/all_gather | solution.py:31
  149.9 4.0 copy-start.1
  153.9 75.3 %copy-start.2 = (s32[512]{0:T(512)S(1)}, s32[512]{0:T(512)}, u32[]{:S(2)}) copy-start(s32[512]{0:T(512)} %param.9) | copy-start | bytes 6148
  153.9 75.3 %copy-start.3 = (f32[512]{0:T(512)S(1)}, f32[512]{0:T(512)}, u32[]{:S(2)}) copy-start(f32[512]{0:T(512)} %param.10) | copy-start | bytes 6148
  157.2 71.9 %all-to-all-start = ((f32[4,32,512]{2,1,0:T(8,128)}), f32[4,32,512]{2,1,0:T(8,128)S(1)}, u32[]{:S(2)}, u32[]{:S(2)}) async-start(f32[4,32,512]{2,1,0:T(8,128)} %broadcast_in_dim.11), calls=%async_computation | async-start | bytes 524288 | tf_op jit(solution)/shard_map/all_to_all | solution.py:44
  161.4 201.9 %all-gather.15.cloned.1.call-start = ((), (), s32[]{:S(2)}) async-start(), calls=%async_computation.4 | async-start | bytes 2621440 | tf_op jit(solution)/shard_map/all_gather | solution.py:31
  372.1 71.9 %all-to-all-start.1 = ((f32[4,32,512]{2,1,0:T(8,128)}), f32[4,32,512]{2,1,0:T(8,128)S(1)}, u32[]{:S(2)}, u32[]{:S(2)}) async-start(f32[4,32,512]{2,1,0:T(8,128)} %broadcast_in_dim.12), calls=%async_computation.1 | async-start | bytes 524288 | tf_op jit(solution)/shard_map/all_to_all | solution.py:44
  376.3 236.4 %all-gather.17.cloned.1.call-start = ((), (), s32[]{:S(2)}) async-start(), calls=%async_computation.5 | async-start | bytes 2621440 | tf_op jit(solution)/shard_map/all_gather | solution.py:31
  621.4 8.8 %all-to-all-start.2 = ((f32[4,32,512]{2,1,0:T(8,128)}), f32[4,32,512]{2,1,0:T(8,128)S(1)}, u32[]{:S(2)}, u32[]{:S(2)}) async-start(f32[4,32,512]{2,1,0:T(8,128)} %broadcast_in_dim.13), calls=%async_computation.2 | async-start | bytes 524288 | tf_op jit(solution)/shard_map/all_to_all | solution.py:44
Sparse Core Ops, SparseCore 0:
  115.3 34.5 all-gather.12
  326.6 36.7 all-gather.14
  541.4 36.7 all-gather.16
where the time goes:
time: 712 us; the launch traced here: 711 us
  blocking collectives  548 us (77%)
  waiting for transfers between devices  75.4 us (11%)
  other arithmetic  29.6 us (4%)
  matrix products  19.3 us (3%)
  between operations  14.2 us (2%)
  local copies, waits for them, and re-layouts  12 us (2%)
  starting transfers between devices  12 us (2%)
    psum x35, blocking collectives, one_axis_at_a_time(): shard = lax.psum(shard, axis)  468 us
    all_gather x6, blocking collectives, all_blocks(): parts = lax.all_gather(parts, axes[k])  79.7 us
    all_gather x3, waiting for transfers between devices, all_blocks(): parts = lax.all_gather(parts, axes[k])  70.1 us
    dot_general x3, matrix products, local(): lax.dot_general(col_block, operator, (((1,), (1,)), ((), ())), preferred_...  14.6 us
  transfers between devices with their start and end apart: 6, of which 3 were waited for; matrix products, arithmetic and copies ran while one was open for 0% of the time, Pallas kernels for 0%

commit v1 on v0

v1 whole, which is shorter than its diff:
```python
import jax
import jax.numpy as jnp
from jax import lax
from jax.experimental import pallas as pl
from jax.experimental.pallas import tpu as pltpu
from jax.sharding import Mesh
from jax.sharding import PartitionSpec as P

N = 32768
S = 32
BODIES = 64
STEPS = 3
ROWS = 512
COLS = 8192
Q = 128
AXES = ("y", "xh", "z", "xl", "co")
ROW = ("y", "xh", "z")
COL = ("xl", "co")
MESH = pl.DeviceIdType.MESH
F32 = jnp.float32
BF16 = jnp.bfloat16
OP_CHUNKS = 4
MM_CHUNK = 2048


def mm(a, b):
    return lax.dot_general(
        a, b, (((1,), (0,)), ((), ())), precision=lax.Precision.HIGHEST, preferred_element_type=F32
    )


def mm_t(a, b):
    return lax.dot_general(
        a, b, (((1,), (1,)), ((), ())), precision=lax.Precision.HIGHEST, preferred_element_type=F32
    )


def factor(gram):
    row_id = lax.broadcasted_iota(jnp.int32, (S, Q), 0)
    lane_id = lax.broadcasted_iota(jnp.int32, (S, Q), 1)
    eye = (lane_id == row_id + S).astype(F32)
    work = jnp.concatenate([gram, jnp.zeros((S, Q - S), F32)], axis=1) + eye
    for k in range(S):
        pivot = work[k : k + 1, k : k + 1]
        r = lax.rsqrt(pivot)
        r = r * (1.5 - 0.5 * pivot * r * r)
        row = work[k : k + 1, :] * r
        col = work[:, k : k + 1] * r
        update = jnp.where(row_id > k, work - col * row, work)
        work = jnp.where(row_id == k, row, update)
    upper = jnp.where(lane_id >= row_id, work, 0.0)[:, :S]
    return upper, work[:, S : 2 * S]


def kernel(
    op_hbm,
    rhs_ref,
    bodies_ref,
    weights_ref,
    basis_ref,
    hess_ref,
    start_ref,
    op,
    stack,
    images,
    means,
    low,
    gathered,
    part,
    parts_in,
    pay0,
    pay1,
    half_in,
    z_buf,
    x_buf,
    y_buf,
    total,
    op_sem,
    g_send,
    g_recv,
    r_send,
    r_recv,
    a_send,
    a_recv,
):
    y, xh, z, xl, co = (lax.axis_index(a) for a in AXES)
    c = xl * 2 + co
    x = xh * 2 + xl
    mine = ((xh * 8 + z) * 4 + c) * Q
    holds = jnp.logical_and(xl == y // 2, co == y % 2)

    loads = []
    width = COLS // OP_CHUNKS
    for i in range(OP_CHUNKS):
        window = pl.ds(i * width, width)
        loads.append(pltpu.make_async_copy(op_hbm.at[:, window], op.at[:, window], op_sem.at[i]))
        loads[-1].start()

    def gather_to(i):
        return ((y + i % 4) % 4, (xh + (i // 4) % 2) % 2, (z + i // 8) % 8, y // 2, y % 2)

    def gather_from(i):
        return (c, i // 32, (i // 4) % 8, (i // 2) % 2, i % 2)

    def z_peer(i):
        return (y, xh, (z + i) % 8, xl, co)

    def x_peer(i):
        t = (x + i) % 4
        return (y, t // 2, z, t % 2, co)

    def y_peer(i):
        return ((y + i) % 4, xh, z, xl, co)

    def col_peer(i):
        t = (c + i) % 4
        return (y, xh, z, t // 2, t % 2)

    other_core = (y, xh, z, xl, 1 - co)

    barrier = pltpu.get_barrier_semaphore()

    def greet(count, peer, first):
        def body(i, carry):
            pl.semaphore_signal(barrier, inc=1, device_id=peer(i), device_id_type=MESH)
            return carry

        lax.fori_loop(first, count, body, 0)
        return count - first

    greeted = greet(64, gather_to, 0)
    greeted += greet(64, gather_from, 0)
    greeted += greet(8, z_peer, 1)
    greeted += greet(4, x_peer, 1)
    greeted += greet(4, y_peer, 1)
    greeted += greet(4, col_peer, 1)

    quarter = pl.ds(pl.multiple_of(c * Q, Q), Q)
    weight = weights_ref[:, quarter]
    body = bodies_ref[:, quarter]
    ids = lax.broadcasted_iota(jnp.int32, (BODIES, Q), 0)
    stack[pl.ds(0, BODIES), :] = jnp.where(ids == body, weight, 0.0)
    stack[pl.ds(BODIES, 4 * S), :] = jnp.zeros((4 * S, Q), F32)
    means[...] = jnp.zeros_like(means)
    hess_ref[...] = jnp.zeros_like(hess_ref)
    images[...] = jnp.zeros_like(images)
    newest = rhs_ref[:, quarter]

    pl.semaphore_wait(barrier, greeted)

    pending = []

    def remote(src, dst, send, recv, device):
        return pltpu.make_async_remote_copy(
            src_ref=src, dst_ref=dst, send_sem=send, recv_sem=recv, device_id=device, device_id_type=MESH
        )

    def await_bytes(ref, sem):
        pltpu.make_async_copy(ref, ref, sem).wait()

    def reduced(j, pay):
        rows = pay.shape[0]
        h = rows // 2
        mine_rows = pl.ds(pl.multiple_of(co * h, h), h)
        theirs = pl.ds(pl.multiple_of((1 - co) * h, h), h)
        part_in = half_in.at[j, pl.ds(0, h), :]
        remote(pay.at[theirs, :], part_in, a_send.at[j, 0], a_recv.at[j, 0], other_core).start()
        pending.append((pay.at[theirs, :], a_send.at[j, 0], 1))
        await_bytes(part_in, a_recv.at[j, 0])
        value = pay[mine_rows, :] + half_in[j, :h, :]
        for stage, (buf, here, count, peer) in enumerate(
            ((z_buf, z, 8, z_peer), (x_buf, x, 4, x_peer), (y_buf, y, 4, y_peer))
        ):
            slot = buf.at[j, here, pl.ds(0, h), :]
            buf[j, here, pl.ds(0, h), :] = value
            for i in range(1, count):
                remote(slot, slot, a_send.at[j, 1 + stage], a_recv.at[j, 1 + stage], peer(i)).start()
            pending.append((buf.at[j, pl.ds(0, count - 1), pl.ds(0, h), :], a_send.at[j, 1 + stage], 1))
            await_bytes(buf.at[j, pl.ds(0, count - 1), pl.ds(0, h), :], a_recv.at[j, 1 + stage])
            value = buf[j, 0, :h, :]
            for i in range(1, count):
                value = value + buf[j, i, :h, :]
        total[j, mine_rows, :] = value
        out = total.at[j, mine_rows, :]
        remote(out, out, a_send.at[j, 4], a_recv.at[j, 4], other_core).start()
        pending.append((out, a_send.at[j, 4], 1))
        await_bytes(total.at[j, theirs, :], a_recv.at[j, 4])

    pred = None
    for j in range(STEPS + 1):
        last = j == STEPS
        stack[pl.ds(BODIES + S * j, S), :] = newest
        if not last:
            low[j] = newest.astype(BF16)
            slot = gathered.at[j, :, pl.ds(pl.multiple_of(mine, Q), Q)]

            def send(i, carry):
                own = jnp.logical_and(i == 0, holds)

                @pl.when(jnp.logical_not(own))
                def _():
                    remote(low.at[j], slot, g_send.at[j], g_recv.at[j], gather_to(i)).start()

                @pl.when(own)
                def _():
                    pltpu.make_async_copy(low.at[j], slot, g_recv.at[j]).start()

                return carry

            lax.fori_loop(0, 64, send, 0)
        if last:
            pay0[j] = mm_t(newest, stack[pl.ds(BODIES, 4 * S), :])
            pay = pay0.at[j]
        elif j == 2:
            pay1[pl.ds(0, S), :] = mm_t(newest, stack[pl.ds(0, Q), :])
            pay1[pl.ds(S, S), :] = jnp.concatenate(
                [mm_t(newest, newest), jnp.zeros((S, Q - S), F32)], axis=1
            )
            pay = pay1
        else:
            pay0[j] = mm_t(newest, stack[pl.ds(0, Q), :])
            pay = pay0.at[j]
        reduced(j, pay)
        sums = total[j, :S, :] * (1.0 / N)
        if last:
            coef, gram = sums[:, : 3 * S], sums[:, 3 * S :]
        elif j == 2:
            coef, gram = sums[:, BODIES:], total[j, S : 2 * S, :S] * (1.0 / N)
        elif j == 1:
            coef, gram = sums[:, BODIES : BODIES + S], sums[:, BODIES + S :]
        else:
            coef, gram = None, sums[:, BODIES : BODIES + S]
        if coef is not None:
            gram = gram - mm_t(coef, coef)
        upper, inverse = factor(gram)
        if j == 0:
            start_ref[...] = upper.T
        else:
            full = coef + pred
            full = jnp.concatenate([full, jnp.zeros((S, Q - S * j), F32)], axis=1)
            hess_ref[pl.ds(0, S * j), pl.ds(S * (j - 1), S)] = full.T[: S * j, :]
            hess_ref[pl.ds(S * j, S), pl.ds(S * (j - 1), S)] = upper
        before = pl.ds(BODIES, S * j)
        upto = pl.ds(BODIES, S * (j + 1))
        residual = newest
        if j > 0:
            residual = residual - mm(coef, stack[before, :])
        vector = mm(inverse, residual)
        stack[pl.ds(BODIES + S * j, S), :] = vector
        basis_ref[pl.ds(S * j, S), :] = vector
        if last:
            break
        mean = sums[:, :BODIES] * BODIES
        raw = 0.5 * newest + mm(mean, stack[pl.ds(0, BODIES), :])
        mean = jnp.concatenate([mean, jnp.zeros((S, Q - BODIES), F32)], axis=1)
        if j > 0:
            mean = mean - mm(coef, means[pl.ds(0, S * j), :])
            raw = raw - mm(coef, images[pl.ds(0, S * j), :])
        mean = mm(inverse, mean)
        means[pl.ds(S * j, S), :] = mean
        lane = lax.broadcasted_iota(jnp.int32, (S, S * (j + 1)), 1)
        sub = lax.broadcasted_iota(jnp.int32, (S, S * (j + 1)), 0)
        pred = mm_t(mean, means[pl.ds(0, S * (j + 1)), :]) * (1.0 / BODIES)
        pred = pred + jnp.where(lane == sub + S * j, 0.5, 0.0)
        raw = mm(inverse, raw)
        shifted = mm(pred, stack[upto, :])

        if j == 0:
            for load in loads:
                load.wait()
        await_bytes(gathered.at[j], g_recv.at[j])
        acc = jnp.zeros((S, ROWS), F32)
        for i in range(COLS // MM_CHUNK):
            acc = acc + lax.dot_general(
                gathered[j, :, i * MM_CHUNK : (i + 1) * MM_CHUNK],
                op[:, i * MM_CHUNK : (i + 1) * MM_CHUNK],
                (((1,), (1,)), ((), ())),
                preferred_element_type=F32,
            )
        for i in range(4):
            part[j, i] = acc[:, i * Q : (i + 1) * Q]
        parts_in[j, c] = part[j, c]
        for i in range(1, 4):
            remote(part.at[j, (c + i) % 4], parts_in.at[j, c], r_send.at[j], r_recv.at[j], col_peer(i)).start()
        pending.append((part.at[j, pl.ds(0, 3)], r_send.at[j], 1))
        await_bytes(parts_in.at[j, pl.ds(0, 3)], r_recv.at[j])
        coupled = parts_in[j, 0] + parts_in[j, 1] + parts_in[j, 2] + parts_in[j, 3]
        image = mm(inverse, coupled) + raw
        images[pl.ds(S * j, S), :] = image
        newest = image - shifted

    for j in range(STEPS):

        def sent(i, carry):
            @pl.when(jnp.logical_not(jnp.logical_and(i == 0, holds)))
            def _():
                await_bytes(low.at[j], g_send.at[j])

            return carry

        lax.fori_loop(0, 64, sent, 0)
    for ref, sem, _ in pending:
        await_bytes(ref, sem)


def local(operator, rhs, bodies, weights):
    vmem = pl.BlockSpec(memory_space=pltpu.VMEM)
    dma = pltpu.SemaphoreType.DMA
    return pl.pallas_call(
        kernel,
        name="arnoldi",
        out_shape=(
            jax.ShapeDtypeStruct((4 * S, Q), F32),
            jax.ShapeDtypeStruct((4 * S, 3 * S), F32),
            jax.ShapeDtypeStruct((S, S), F32),
        ),
        in_specs=[pl.BlockSpec(memory_space=pl.ANY), vmem, vmem, vmem],
        out_specs=(vmem, vmem, vmem),
        scratch_shapes=[
            pltpu.VMEM((ROWS, COLS), BF16),
            pltpu.VMEM((BODIES + 4 * S, Q), F32),
            pltpu.VMEM((3 * S, Q), F32),
            pltpu.VMEM((3 * S, Q), F32),
            pltpu.VMEM((3, S, Q), BF16),
            pltpu.VMEM((3, S, COLS), BF16),
            pltpu.VMEM((3, 4, S, Q), F32),
            pltpu.VMEM((3, 4, S, Q), F32),
            pltpu.VMEM((4, S, Q), F32),
            pltpu.VMEM((2 * S, Q), F32),
            pltpu.VMEM((4, S, Q), F32),
            pltpu.VMEM((4, 8, S, Q), F32),
            pltpu.VMEM((4, 4, S, Q), F32),
            pltpu.VMEM((4, 4, S, Q), F32),
            pltpu.VMEM((4, 2 * S, Q), F32),
            dma((OP_CHUNKS,)),
            dma((3,)),
            dma((3,)),
            dma((3,)),
            dma((3,)),
            dma((4, 5)),
            dma((4, 5)),
        ],
        compiler_params=pltpu.CompilerParams(
            collective_id=0, has_side_effects=True, vmem_limit_bytes=40 * 2**20
        ),
    )(operator, rhs, bodies.reshape(1, ROWS), weights.reshape(1, ROWS))


def solution(mesh):
    split = Mesh(mesh.devices.reshape(4, 2, 8, 2, 2), AXES)
    placed = (P(ROW, COL), P(None, ROW), P(ROW), P(ROW))
    return jax.shard_map(
        local, mesh=split, in_specs=placed, out_specs=(P(None, ROW + COL), P(), P()), check_vma=False
    )
```

time: 712 us -> 148 us (0.21)
  blocking collectives: 548 us -> 0 us
  Pallas kernels: 0 us -> 139 us
  waiting for transfers between devices: 75.4 us -> 0 us
  other arithmetic: 29.6 us -> 0 us
  matrix products: 19.3 us -> 0 us
  between operations: 14.2 us -> 0.65 us
  starting transfers between devices: 12 us -> 0 us
    psum x35 -> x0, blocking collectives: 468 us -> none  [one_axis_at_a_time(): shard = lax.psum(shard, axis)]
    pallas_call x0 -> x1, Pallas kernels: none -> 139 us  [local(): pl.pallas_call(kernel, name='arnoldi', out_shape=(jax.ShapeDtypeStruct((4...]
    all_gather x6 -> x0, blocking collectives: 79.7 us -> none  [all_blocks(): parts = lax.all_gather(parts, axes[k])]
    all_gather x3 -> x0, waiting for transfers between devices: 70.1 us -> none  [all_blocks(): parts = lax.all_gather(parts, axes[k])]
    another operation x17 -> x0, other arithmetic: 25.4 us -> none  [the longest x9 10.8 us: local(): factor_low = jnp.linalg.cholesky(gram_block)]
    dot_general x22 -> x0, matrix products: 18.2 us -> none  [the longest x3 14.6 us: local(): lax.dot_general(col_block, operator, (((1,), (1,)), ((), ())), preferred_...]
    all_to_all x3 -> x0, starting transfers between devices: 12 us -> none  [sent_to_all(): return lax.all_to_all(copies, axis, split_axis=0, concat_axis=0, tiled=True)]
  transfers between devices with their start and end apart: 6 -> 0, of which waited for: 3 -> 0; matrix products, arithmetic and copies ran while one was open for 0% -> 0% of each run, Pallas kernels for 0% -> 0%
where the time goes in v1:
time: 148 us; the launch traced here: 147 us
  Pallas kernels  139 us (94%)
  local copies, waits for them, and re-layouts  7.52 us (5%)
    pallas_call x1, Pallas kernels, local(): pl.pallas_call(kernel, name='arnoldi', out_shape=(jax.ShapeDtypeStruct((4...  139 us
    unnamed x10, local copies, waits for them, and re-layouts  6.81 us

profile of v1, /device:TPU:1, one launch (start us, length us, event | category | flops | bytes accessed | tf_op | source)
XLA Modules:
  0.0 147.4 jit_solution(9940322665908920024)
XLA Ops:
  0.6 0.0 copy-start
  0.6 3.4 %copy-done = bf16[512,8192]{1,0:T(8,128)(2,1)S(1)} copy-done((bf16[512,8192]{1,0:T(8,128)(2,1)S(1)}, bf16[512,8192]{1,0:T(8,128)(2,1)}, u32[]{:S(2)}) %copy-start) | copy-done | bytes 8388632
  4.0 0.0 copy-start.1
  4.0 0.8 copy-done.1
  4.9 0.0 copy-start.2
  4.9 0.7 copy-done.2
  5.5 0.0 copy-start.3
  5.5 0.7 copy-done.3
  6.2 139.3 %arnoldi.1 = (f32[128,128]{1,0:T(8,128)S(1)}, f32[128,96]{1,0:T(8,128)S(1)}, f32[32,32]{1,0:T(8,128)S(1)}) custom-call(bf16[512,8192]{1,0:T(8,128)(2,1)S(1)} %copy-done, f32[32,512]{1,0:T(8,128)S(1)} %copy-done.1, s32[1,512]{1,0:T(1,128)S(1)} %bitcast.2, f32[1,512]{1,0:T(1,128)S(1)} %bitcast.3), custom_call_target="tpu_custom_call" | custom-call | tf_op jit(solution)/shard_map/arnoldi/pallas_call | solution.py:309
  145.5 0.7 copy.7
  146.2 0.6 copy.10
  146.8 0.6 copy.11
Async XLA Ops:
  0.6 3.4 %copy-start = (bf16[512,8192]{1,0:T(8,128)(2,1)S(1)}, bf16[512,8192]{1,0:T(8,128)(2,1)}, u32[]{:S(2)}) copy-start(bf16[512,8192]{1,0:T(8,128)(2,1)} %op_hbm.1) | copy-start | bytes 25165828
  4.0 0.8 copy-start.1
  4.9 0.7 copy-start.2
  5.5 0.7 copy-start.3

commit v2 on v1

v2 whole, which is shorter than its diff:
```python
import jax
import jax.numpy as jnp
from jax import lax
from jax.experimental import pallas as pl
from jax.experimental.pallas import tpu as pltpu
from jax.sharding import Mesh
from jax.sharding import PartitionSpec as P

N = 32768
S = 32
BODIES = 64
STEPS = 3
ROWS = 512
COLS = 8192
Q = 128
H = 16
AXES = ("y", "xh", "z", "xl", "co")
ROW = ("y", "xh", "z")
COL = ("xl", "co")
MESH = pl.DeviceIdType.MESH
F32 = jnp.float32
BF16 = jnp.bfloat16
OP_CHUNKS = 4
MM_CHUNK = 2048


def mm(a, b):
    return lax.dot_general(
        a, b, (((1,), (0,)), ((), ())), precision=lax.Precision.HIGHEST, preferred_element_type=F32
    )


def mm_t(a, b):
    return lax.dot_general(
        a, b, (((1,), (1,)), ((), ())), precision=lax.Precision.HIGHEST, preferred_element_type=F32
    )


def dot_low(a, b):
    return lax.dot_general(a, b, (((1,), (1,)), ((), ())), preferred_element_type=F32)


def factor(gram):
    row_id = lax.broadcasted_iota(jnp.int32, (S, Q), 0)
    lane_id = lax.broadcasted_iota(jnp.int32, (S, Q), 1)
    eye = (lane_id == row_id + S).astype(F32)
    work = jnp.concatenate([gram, jnp.zeros((S, Q - S), F32)], axis=1) + eye
    for k in range(S):
        pivot = work[k : k + 1, k : k + 1]
        r = lax.rsqrt(pivot)
        r = r * (1.5 - 0.5 * pivot * r * r)
        row = work[k : k + 1, :] * r
        col = work[:, k : k + 1] * r
        update = jnp.where(row_id > k, work - col * row, work)
        work = jnp.where(row_id == k, row, update)
    upper = jnp.where(lane_id >= row_id, work, 0.0)[:, :S]
    return upper, work[:, S : 2 * S]


def kernel(
    op_hbm,
    rhs_ref,
    bodies_ref,
    weights_ref,
    basis_ref,
    hess_ref,
    start_ref,
    op,
    ext,
    stack,
    wide,
    low,
    mid,
    part,
    parts_in,
    side_out,
    sides_in,
    table_out,
    table_in,
    pay0,
    zc_buf,
    xy_buf,
    total,
    op_sem,
    g_send,
    g0_recv,
    g1_recv,
    gm_recv,
    r_send,
    r_recv,
    s_send,
    s_recv,
    t_sem,
    a_send,
    a_recv,
):
    y, xh, z, xl, co = (lax.axis_index(a) for a in AXES)
    c = xl * 2 + co
    x = xh * 2 + xl
    mine = pl.ds(pl.multiple_of(((xh * 8 + z) * 4 + c) * Q, Q), Q)
    straight = xl == y // 2
    own1 = co == y % 2
    own0 = jnp.logical_and(jnp.logical_and(straight, own1), z % 2 == 0)

    loads = []
    width = COLS // OP_CHUNKS
    for i in range(OP_CHUNKS):
        window = pl.ds(i * width, width)
        loads.append(pltpu.make_async_copy(op_hbm.at[:, window], op.at[:, window], op_sem.at[i]))
        loads[-1].start()

    def plane_to(i):
        return ((y + i % 4) % 4, (xh + (i // 4) % 2) % 2, (z + i // 8) % 8, y // 2, y % 2)

    def plane_from(i):
        return (c, i // 32, (i // 4) % 8, (i // 2) % 2, i % 2)

    def a0_to(i):
        return ((y + 2 * (z % 2)) % 4, (xh + i % 2) % 2, (z + i // 2) % 8, y // 2, y % 2)

    def a0_from(i):
        return (c, i // 16, ((i // 4) % 4) * 2 + ((y + 4 - c) % 4) // 2, (i // 2) % 2, i % 2)

    def a1_to(i):
        return ((y + i % 4) % 4, xh, (z + i // 4) % 8, xl, y % 2)

    def a1_from(i):
        return (co + 2 * (i // 16), xh, (i // 2) % 8, xl, i % 2)

    def zc_peer(i):
        return (y, xh, (z + i // 2) % 8, xl, (co + i) % 2)

    def xy_peer(i):
        t = (x + i) % 4
        return ((y + i // 4) % 4, t // 2, z, t % 2, co)

    def col_peer(i):
        t = (c + i) % 4
        return (y, xh, z, t // 2, t % 2)

    near = z // 4 * 4
    order = ((xh, near), (1 - xh, near), (xh, 4 - near), (1 - xh, 4 - near))
    other_core = (y, xh, z, xl, 1 - co)

    barrier = pltpu.get_barrier_semaphore()

    def greet(count, peer, first):
        def body(i, carry):
            pl.semaphore_signal(barrier, inc=1, device_id=peer(i), device_id_type=MESH)
            return carry

        lax.fori_loop(first, count, body, 0)
        return count - first

    root = (y + 4 - c) % 2 == 0

    @pl.when(root)
    def _():
        greet(32, a0_from, 0)

    greeted = 16 + greet(32, a1_from, 0)
    greeted += greet(64, plane_from, 0)
    greeted += greet(16, zc_peer, 1)
    greeted += greet(16, xy_peer, 1)
    greeted += greet(4, col_peer, 1)

    quarter = pl.ds(pl.multiple_of(c * Q, Q), Q)
    weight = weights_ref[:, quarter]
    body = bodies_ref[:, quarter]
    ids = lax.broadcasted_iota(jnp.int32, (BODIES, Q), 0)
    stack[pl.ds(0, BODIES), :] = jnp.where(ids == body, weight, 0.0)
    stack[pl.ds(BODIES, 4 * S), :] = jnp.zeros((4 * S, Q), F32)
    wide[...] = jnp.zeros_like(wide)
    hess_ref[...] = jnp.zeros_like(hess_ref)
    newest = rhs_ref[:, quarter]
    table_out[pl.ds(0, 1), :] = weight
    table_out[pl.ds(1, 1), :] = body.astype(F32)

    pl.semaphore_wait(barrier, greeted)

    pending = []

    def remote(src, dst, send, recv, device):
        return pltpu.make_async_remote_copy(
            src_ref=src, dst_ref=dst, send_sem=send, recv_sem=recv, device_id=device, device_id_type=MESH
        )

    def await_bytes(ref, sem):
        pltpu.make_async_copy(ref, ref, sem).wait()

    def halves(pay):
        h = pay.shape[0] // 2
        return h, pl.ds(pl.multiple_of(co * h, h), h), pl.ds(pl.multiple_of((1 - co) * h, h), h)

    def sum_start(j, pay):
        h, own, theirs = halves(pay)
        here = z * 2 + co
        zc_buf[j, here, pl.ds(0, h), :] = pay[own, :]
        dst = zc_buf.at[j, here, pl.ds(0, h), :]
        for i in (8, 9, 7, 6, 10, 11, 5, 4, 12, 13, 3, 2, 14, 15, 1):
            src = pay.at[theirs if i % 2 else own, :]
            remote(src, dst, a_send.at[j, 0], a_recv.at[j, 0], zc_peer(i)).start()
        pending.append((zc_buf.at[j, pl.ds(0, 15), pl.ds(0, h), :], a_send.at[j, 0]))

    def summed(buf, j, h, count):
        terms = [buf[j, i, :h, :] for i in range(count)]
        while len(terms) > 1:
            terms = [terms[i] + terms[i + 1] for i in range(0, len(terms), 2)]
        return terms[0]

    def sum_middle(j, pay):
        h, _, _ = halves(pay)
        await_bytes(zc_buf.at[j, pl.ds(0, 15), pl.ds(0, h), :], a_recv.at[j, 0])
        here = y * 4 + x
        xy_buf[j, here, pl.ds(0, h), :] = summed(zc_buf, j, h, 16)
        slot = xy_buf.at[j, here, pl.ds(0, h), :]
        for i in (10, 9, 11, 14, 6, 8, 2, 13, 15, 5, 7, 1, 3, 4, 12):
            remote(slot, slot, a_send.at[j, 1], a_recv.at[j, 1], xy_peer(i)).start()
        pending.append((xy_buf.at[j, pl.ds(0, 15), pl.ds(0, h), :], a_send.at[j, 1]))

    def sum_finish(j, pay):
        h, own, theirs = halves(pay)
        await_bytes(xy_buf.at[j, pl.ds(0, 15), pl.ds(0, h), :], a_recv.at[j, 1])
        total[j, own, :] = summed(xy_buf, j, h, 16)
        out = total.at[j, own, :]
        remote(out, out, a_send.at[j, 2], a_recv.at[j, 2], other_core).start()
        pending.append((out, a_send.at[j, 2]))
        await_bytes(total.at[j, theirs, :], a_recv.at[j, 2])

    def top(j):
        return pl.ds(BODIES + S * j, H)

    def low_rows(j):
        return pl.ds(BODIES + S * j + H, H)

    def all_rows(j):
        return pl.ds(BODIES + S * j, S)


    def lanes0(xh_s, z_s):
        return pl.ds(pl.multiple_of((xh_s * 8 + z_s) * 4 * Q, 4 * Q), 4 * Q)

    def lanes1(x_s, z_s):
        return pl.ds(pl.multiple_of((((x_s // 2) * 8 + z_s) * 2 + x_s % 2) * 2 * Q, 2 * Q), 2 * Q)

    def root_for(z_s):
        return (y + 4 - c) % 4 == 2 * (z_s % 2)

    def loop(first, end, do):
        def body(i, carry):
            do(i)
            return carry

        lax.fori_loop(first, end, body, 0)

    def either(test, yes, no):
        pl.when(test)(yes)
        pl.when(jnp.logical_not(test))(no)

    def gather_start(j):
        src1, src0 = low.at[j, pl.ds(H, H), :], low.at[j, pl.ds(0, H), :]
        at1 = ext.at[low_rows(j), mine]
        at_mid = mid.at[j, z, :, pl.ds(pl.multiple_of(co * Q, Q), Q)]
        at0 = ext.at[top(j), mine]
        sem1, sem_mid, sem0 = g1_recv.at[j, x * 8 + z], gm_recv.at[j, z], g0_recv.at[j, xh * 8 + z]

        def spread1(dst, sem):
            loop(4, 32, lambda i: remote(src1, dst, g_send.at[j, 1], sem, a1_to(i)).start())
            loop(1, 4, lambda i: remote(src1, dst, g_send.at[j, 1], sem, a1_to(i)).start())
            either(
                own1,
                lambda: pltpu.make_async_copy(src1, dst, sem).start(),
                lambda: remote(src1, dst, g_send.at[j, 1], sem, a1_to(0)).start(),
            )

        either(straight, lambda: spread1(at1, sem1), lambda: spread1(at_mid, sem_mid))
        loop(1, 16, lambda i: remote(src0, at0, g_send.at[j, 0], sem0, a0_to(i)).start())
        either(
            own0,
            lambda: pltpu.make_async_copy(src0, at0, sem0).start(),
            lambda: remote(src0, at0, g_send.at[j, 0], sem0, a0_to(0)).start(),
        )

    def relay(j, d):
        z_s = (z + d) % 8
        here = ext.at[low_rows(j), lanes1(x, z_s)]
        sem1 = g1_recv.at[j, x * 8 + z_s]
        await_bytes(here, sem1)
        remote(here, here, g_send.at[j, 2], sem1, (y, 1 - xh, z, xl, co)).start()
        held = mid.at[j, z_s]
        await_bytes(held, gm_recv.at[j, z_s])
        for t in range(2):
            remote(held, here, g_send.at[j, 2], sem1, (y, t, z, 1 - xl, co)).start()

        @pl.when(root_for(z_s))
        def _():
            for xh_s in range(2):
                block = ext.at[top(j), lanes0(xh_s, z_s)]
                sem0 = g0_recv.at[j, xh_s * 8 + z_s]
                await_bytes(block, sem0)
                for i in (2, 1, 3):
                    remote(block, block, g_send.at[j, 3], sem0, ((y + i) % 4, xh, z, xl, co)).start()

    def await_chunk(j, xh_s, z_first):
        def one(k):
            z_s = z_first + k

            @pl.when(jnp.logical_not(root_for(z_s)))
            def _():
                await_bytes(ext.at[top(j), lanes0(xh_s, z_s)], g0_recv.at[j, xh_s * 8 + z_s])

            for xl_s in range(2):
                x_s = xh_s * 2 + xl_s

                @pl.when(x_s != x)
                def _():
                    await_bytes(ext.at[low_rows(j), lanes1(x_s, z_s)], g1_recv.at[j, x_s * 8 + z_s])

        loop(0, 4, one)

    def gather_sent(j):
        either(
            own0,
            lambda: await_bytes(ext.at[top(j), pl.ds(0, 15 * Q)], g_send.at[j, 0]),
            lambda: await_bytes(ext.at[top(j), pl.ds(0, 16 * Q)], g_send.at[j, 0]),
        )
        either(
            own1,
            lambda: await_bytes(ext.at[top(j), pl.ds(0, 31 * Q)], g_send.at[j, 1]),
            lambda: await_bytes(ext.at[top(j), pl.ds(0, 32 * Q)], g_send.at[j, 1]),
        )
        await_bytes(ext.at[top(j), pl.ds(0, 48 * Q)], g_send.at[j, 2])

        @pl.when(root)
        def _():
            await_bytes(ext.at[all_rows(j), pl.ds(0, 48 * Q)], g_send.at[j, 3])

    here = xh * 32 + z * 4 + c
    tables = pl.ds(0, 2)

    def table_start():
        src, dst = table_out.at[tables, :], table_in.at[here, tables, :]
        loop(1, 64, lambda i: remote(src, dst, t_sem.at[0], t_sem.at[1], plane_to(i)).start())
        either(
            jnp.logical_and(straight, own1),
            lambda: pltpu.make_async_copy(src, dst, t_sem.at[1]).start(),
            lambda: remote(src, dst, t_sem.at[0], t_sem.at[1], plane_to(0)).start(),
        )

    def table_finish():
        await_bytes(table_in.at[:, tables, :], t_sem.at[1])

        def build(i):
            plane = jnp.where(ids.astype(F32) == table_in[i, 1:2, :], table_in[i, 0:1, :], 0.0)
            ext[pl.ds(0, BODIES), pl.ds(pl.multiple_of(i * Q, Q), Q)] = plane.astype(BF16)

        loop(0, 64, build)

    def padded(value):
        return jnp.concatenate([value, jnp.zeros((S, Q - value.shape[1]), F32)], axis=1)

    lane = lax.broadcasted_iota(jnp.int32, (S, Q), 1)
    sub = lax.broadcasted_iota(jnp.int32, (S, Q), 0)
    pred = None

    def write_hess(j, coef, upper):
        full = padded(coef + pred).T
        hess_ref[pl.ds(0, S * j), pl.ds(S * (j - 1), S)] = full[: S * j, :]
        hess_ref[pl.ds(S * j, S), pl.ds(S * (j - 1), S)] = upper

    for j in range(STEPS):
        low[j] = newest.astype(BF16)
        gather_start(j)
        if j == 0:
            table_start()
        elif j == 1:
            start_ref[...] = upper.T
        else:
            write_hess(j - 1, coef, upper)
        if j > 0:
            pred = next_pred
        for d in (0, 1, 7, 2, 6, 3, 5, 4):
            relay(j, d)
        if j == 0:
            table_finish()
            for load in loads:
                load.wait()
        acc, side = None, None
        for i in range(4):
            xh_s, z_first = order[i]
            window = pl.ds(pl.multiple_of((xh_s * 8 + z_first) * 4 * Q, MM_CHUNK), MM_CHUNK)
            await_chunk(j, xh_s, z_first)
            term = dot_low(ext[all_rows(j), window], op[:, window])
            acc = term if acc is None else acc + term
            term = dot_low(ext[all_rows(j), window], ext[pl.ds(0, BODIES + S * (j + 1)), window])
            side = term if side is None else side + term
        for i in range(4):
            part[j, i] = acc[:, i * Q : (i + 1) * Q]
        for i in range(1, 4):
            remote(part.at[j, (c + i) % 4], parts_in.at[j, c], r_send.at[j], r_recv.at[j], col_peer(i)).start()
        pending.append((part.at[j, pl.ds(0, 3)], r_send.at[j]))
        parts_in[j, c] = part[j, c]
        blocks = 2 if j == 2 else 1
        side_out[j, 0] = padded(side[:, :Q]) if j < 1 else side[:, :Q]
        if blocks == 2:
            side_out[j, 1] = padded(side[:, Q:])
        out = side_out.at[j, pl.ds(0, blocks)]
        for i in range(1, 4):
            remote(out, sides_in.at[j, c, pl.ds(0, blocks)], s_send.at[j], s_recv.at[j], col_peer(i)).start()
        pending.append((sides_in.at[j, pl.ds(0, 3), pl.ds(0, blocks)], s_send.at[j]))
        for k in range(blocks):
            sides_in[j, c, k] = side_out[j, k]
        await_bytes(sides_in.at[j, pl.ds(0, 3), pl.ds(0, blocks)], s_recv.at[j])
        sums = [
            (sides_in[j, 0, k] + sides_in[j, 1, k]) + (sides_in[j, 2, k] + sides_in[j, 3, k]) for k in range(blocks)
        ]
        mean = sums[0][:, :BODIES] * (BODIES / N)
        raw = sums[0][:, BODIES:] * (1.0 / N)
        if j == 2:
            raw = jnp.concatenate([raw, sums[1][:, :S] * (1.0 / N)], axis=1)
        gram = raw[:, S * j : S * (j + 1)]
        coef = None
        if j > 0:
            coef = mm_t(padded(raw[:, : S * j]), wide[pl.ds(0, S * j), pl.ds(3 * Q, Q)])
            gram = gram - mm_t(coef, coef)
        upper, inverse = factor(gram)
        completion = mm(mean, stack[pl.ds(0, BODIES), :])
        await_bytes(parts_in.at[j, pl.ds(0, 3)], r_recv.at[j])
        coupled = (parts_in[j, 0] + parts_in[j, 1]) + (parts_in[j, 2] + parts_in[j, 3])
        image = 0.5 * newest + completion + coupled
        full = jnp.concatenate([newest, image, padded(mean), jnp.where(lane == sub + S * j, 1.0, 0.0)], axis=1)
        if j > 0:
            full = full - mm(coef, wide[pl.ds(0, S * j), :])
        full = mm(inverse, full)
        wide[pl.ds(S * j, S), :] = full
        upto = pl.ds(0, S * (j + 1))
        next_pred = mm_t(full[:, 2 * Q : 3 * Q], wide[upto, pl.ds(2 * Q, Q)]) * (1.0 / BODIES)
        next_pred = next_pred + jnp.where(lane == sub + S * j, 0.5, 0.0)[:, : S * (j + 1)]
        newest = full[:, Q : 2 * Q] - mm(next_pred, wide[upto, pl.ds(0, Q)])

    for j in range(STEPS):
        basis_ref[pl.ds(S * j, S), :] = wide[pl.ds(S * j, S), pl.ds(0, Q)]
        stack[pl.ds(BODIES + S * j, S), :] = wide[pl.ds(S * j, S), pl.ds(0, Q)]
    stack[pl.ds(BODIES + S * STEPS, S), :] = newest
    pay0[...] = mm_t(newest, stack[pl.ds(BODIES, 4 * S), :])
    sum_start(0, pay0)
    write_hess(2, coef, upper)
    pred = next_pred
    for i in range(STEPS):
        gather_sent(i)
    either(
        jnp.logical_and(straight, own1),
        lambda: await_bytes(table_in.at[pl.ds(0, 63), tables, :], t_sem.at[0]),
        lambda: await_bytes(table_in.at[:, tables, :], t_sem.at[0]),
    )
    sum_middle(0, pay0)
    sum_finish(0, pay0)
    sums = total[0] * (1.0 / N)
    coef, gram = sums[:, : 3 * S], sums[:, 3 * S :]
    gram = gram - mm_t(coef, coef)
    residual = newest - mm(coef, stack[pl.ds(BODIES, 3 * S), :])
    upper, inverse = factor(gram)
    basis_ref[pl.ds(3 * S, S), :] = mm(inverse, residual)
    write_hess(3, coef, upper)

    for ref, sem in pending:
        await_bytes(ref, sem)


def local(operator, rhs, bodies, weights):
    vmem = pl.BlockSpec(memory_space=pltpu.VMEM)
    dma = pltpu.SemaphoreType.DMA
    return pl.pallas_call(
        kernel,
        name="arnoldi",
        out_shape=(
            jax.ShapeDtypeStruct((4 * S, Q), F32),
            jax.ShapeDtypeStruct((4 * S, 3 * S), F32),
            jax.ShapeDtypeStruct((S, S), F32),
        ),
        in_specs=[pl.BlockSpec(memory_space=pl.ANY), vmem, vmem, vmem],
        out_specs=(vmem, vmem, vmem),
        scratch_shapes=[
            pltpu.VMEM((ROWS, COLS), BF16),
            pltpu.VMEM((BODIES + 3 * S, COLS), BF16),
            pltpu.VMEM((BODIES + 4 * S, Q), F32),
            pltpu.VMEM((3 * S, 4 * Q), F32),
            pltpu.VMEM((3, S, Q), BF16),
            pltpu.VMEM((3, 8, H, 2 * Q), BF16),
            pltpu.VMEM((3, 4, S, Q), F32),
            pltpu.VMEM((3, 4, S, Q), F32),
            pltpu.VMEM((3, 2, S, Q), F32),
            pltpu.VMEM((3, 4, 2, S, Q), F32),
            pltpu.VMEM((8, Q), F32),
            pltpu.VMEM((64, 8, Q), F32),
            pltpu.VMEM((S, Q), F32),
            pltpu.VMEM((1, 16, H, Q), F32),
            pltpu.VMEM((1, 16, H, Q), F32),
            pltpu.VMEM((1, S, Q), F32),
            dma((OP_CHUNKS,)),
            dma((3, 4)),
            dma((3, 16)),
            dma((3, 32)),
            dma((3, 8)),
            dma((3,)),
            dma((3,)),
            dma((3,)),
            dma((3,)),
            dma((2,)),
            dma((1, 3)),
            dma((1, 3)),
        ],
        compiler_params=pltpu.CompilerParams(
            collective_id=0, has_side_effects=True, vmem_limit_bytes=40 * 2**20
        ),
    )(operator, rhs, bodies.reshape(1, ROWS), weights.reshape(1, ROWS))


def solution(mesh):
    split = Mesh(mesh.devices.reshape(4, 2, 8, 2, 2), AXES)
    placed = (P(ROW, COL), P(None, ROW), P(ROW), P(ROW))
    return jax.shard_map(
        local, mesh=split, in_specs=placed, out_specs=(P(None, ROW + COL), P(), P()), check_vma=False
    )
```

time: 148 us -> 118 us (0.80)
  Pallas kernels: 139 us -> 110 us
    pallas_call x1, Pallas kernels: 139 us -> 110 us  [local(): pl.pallas_call(kernel, name='arnoldi', out_shape=(jax.ShapeDtypeStruct((4...]
where the time goes in v2:
time: 118 us
  Pallas kernels  110 us (93%)
  local copies, waits for them, and re-layouts  7.52 us (6%)
    pallas_call x1, Pallas kernels, local(): pl.pallas_call(kernel, name='arnoldi', out_shape=(jax.ShapeDtypeStruct((4...  110 us
    unnamed x10, local copies, waits for them, and re-layouts  6.81 us

profile of v2, /device:TPU:1, one launch (start us, length us, event | category | flops | bytes accessed | tf_op | source)
XLA Modules:
  0.0 117.7 jit_solution(14862706586931672884)
XLA Ops:
  0.6 0.0 copy-start
  0.6 3.4 %copy-done = bf16[512,8192]{1,0:T(8,128)(2,1)S(1)} copy-done((bf16[512,8192]{1,0:T(8,128)(2,1)S(1)}, bf16[512,8192]{1,0:T(8,128)(2,1)}, u32[]{:S(2)}) %copy-start) | copy-done | bytes 8388632
  4.0 0.0 copy-start.1
  4.0 0.8 copy-done.1
  4.9 0.0 copy-start.2
  4.9 0.7 copy-done.2
  5.5 0.0 copy-start.3
  5.5 0.7 copy-done.3
  6.2 109.6 %arnoldi.1 = (f32[128,128]{1,0:T(8,128)S(1)}, f32[128,96]{1,0:T(8,128)S(1)}, f32[32,32]{1,0:T(8,128)S(1)}) custom-call(bf16[512,8192]{1,0:T(8,128)(2,1)S(1)} %copy-done, f32[32,512]{1,0:T(8,128)S(1)} %copy-done.1, s32[1,512]{1,0:T(1,128)S(1)} %bitcast.2, f32[1,512]{1,0:T(1,128)S(1)} %bitcast.3), custom_call_target="tpu_custom_call" | custom-call | tf_op jit(solution)/shard_map/arnoldi/pallas_call | solution.py:473
  115.8 0.7 copy.7
  116.5 0.6 copy.10
  117.1 0.6 copy.11
Async XLA Ops:
  0.6 3.4 %copy-start = (bf16[512,8192]{1,0:T(8,128)(2,1)S(1)}, bf16[512,8192]{1,0:T(8,128)(2,1)}, u32[]{:S(2)}) copy-start(bf16[512,8192]{1,0:T(8,128)(2,1)} %op_hbm.1) | copy-start | bytes 25165828
  4.0 0.8 copy-start.1
  4.9 0.7 copy-start.2
  5.5 0.7 copy-start.3

commit v3 on v2

--- a/solution.py
+++ b/solution.py
@@ -21,7 +21,7 @@
 F32 = jnp.float32
 BF16 = jnp.bfloat16
 OP_CHUNKS = 4
-MM_CHUNK = 2048
+NEAR = (0, 1, 7, 2, 6, 3, 5, 4)
 
 
 def mm(a, b):
@@ -45,14 +45,13 @@
     lane_id = lax.broadcasted_iota(jnp.int32, (S, Q), 1)
     eye = (lane_id == row_id + S).astype(F32)
     work = jnp.concatenate([gram, jnp.zeros((S, Q - S), F32)], axis=1) + eye
-    for k in range(S):
-        pivot = work[k : k + 1, k : k + 1]
-        r = lax.rsqrt(pivot)
-        r = r * (1.5 - 0.5 * pivot * r * r)
-        row = work[k : k + 1, :] * r
-        col = work[:, k : k + 1] * r
-        update = jnp.where(row_id > k, work - col * row, work)
-        work = jnp.where(row_id == k, row, update)
+    for k in range(S - 1):
+        col = jnp.broadcast_to(work[:, k : k + 1], (S, Q))
+        share = jnp.where(row_id > k, col * work[k : k + 1, :], 0.0)
+        work = work - share * (1.0 / col[k : k + 1, :])
+    pivots = jnp.sum(jnp.where(lane_id == row_id, work, 0.0), axis=1, keepdims=True)
+    r = lax.rsqrt(pivots)
+    work = work * (r * (1.5 - 0.5 * pivots * r * r))
     upper = jnp.where(lane_id >= row_id, work, 0.0)[:, :S]
     return upper, work[:, S : 2 * S]
 
@@ -75,6 +74,8 @@
     parts_in,
     side_out,
     sides_in,
+    acc,
+    side_acc,
     table_out,
     table_in,
     pay0,
@@ -138,8 +139,6 @@
         t = (c + i) % 4
         return (y, xh, z, t // 2, t % 2)
 
-    near = z // 4 * 4
-    order = ((xh, near), (1 - xh, near), (xh, 4 - near), (1 - xh, 4 - near))
     other_core = (y, xh, z, xl, 1 - co)
 
     barrier = pltpu.get_barrier_semaphore()
@@ -228,14 +227,13 @@
         await_bytes(total.at[j, theirs, :], a_recv.at[j, 2])
 
     def top(j):
-        return pl.ds(BODIES + S * j, H)
+        return pl.ds(2 * BODIES + S * j, H)
 
     def low_rows(j):
-        return pl.ds(BODIES + S * j + H, H)
+        return pl.ds(2 * BODIES + S * j + H, H)
 
     def all_rows(j):
-        return pl.ds(BODIES + S * j, S)
-
+        return pl.ds(2 * BODIES + S * j, S)
 
     def lanes0(xh_s, z_s):
         return pl.ds(pl.multiple_of((xh_s * 8 + z_s) * 4 * Q, 4 * Q), 4 * Q)
@@ -301,22 +299,15 @@
                 for i in (2, 1, 3):
                     remote(block, block, g_send.at[j, 3], sem0, ((y + i) % 4, xh, z, xl, co)).start()
 
-    def await_chunk(j, xh_s, z_first):
-        def one(k):
-            z_s = z_first + k
-
-            @pl.when(jnp.logical_not(root_for(z_s)))
-            def _():
+    def await_z(j, z_s):
+        @pl.when(jnp.logical_not(root_for(z_s)))
+        def _():
+            for xh_s in range(2):
                 await_bytes(ext.at[top(j), lanes0(xh_s, z_s)], g0_recv.at[j, xh_s * 8 + z_s])
 
-            for xl_s in range(2):
-                x_s = xh_s * 2 + xl_s
-
-                @pl.when(x_s != x)
-                def _():
-                    await_bytes(ext.at[low_rows(j), lanes1(x_s, z_s)], g1_recv.at[j, x_s * 8 + z_s])
-
-        loop(0, 4, one)
+        for i in range(1, 4):
+            x_s = (x + i) % 4
+            await_bytes(ext.at[low_rows(j), lanes1(x_s, z_s)], g1_recv.at[j, x_s * 8 + z_s])
 
     def gather_sent(j):
         either(
@@ -352,7 +343,10 @@
 
         def build(i):
             plane = jnp.where(ids.astype(F32) == table_in[i, 1:2, :], table_in[i, 0:1, :], 0.0)
-            ext[pl.ds(0, BODIES), pl.ds(pl.multiple_of(i * Q, Q), Q)] = plane.astype(BF16)
+            window = pl.ds(pl.multiple_of(i * Q, Q), Q)
+            high = plane.astype(BF16)
+            ext[pl.ds(0, BODIES), window] = high
+            ext[pl.ds(BODIES, BODIES), window] = (plane - high.astype(F32)).astype(BF16)
 
         loop(0, 64, build)
 
@@ -379,45 +373,54 @@
             write_hess(j - 1, coef, upper)
         if j > 0:
             pred = next_pred
-        for d in (0, 1, 7, 2, 6, 3, 5, 4):
+        for d in NEAR:
             relay(j, d)
         if j == 0:
             table_finish()
             for load in loads:
                 load.wait()
-        acc, side = None, None
+        for n, d in enumerate(NEAR):
+            z_s = (z + d) % 8
+            await_z(j, z_s)
+            pair = (lanes0(0, z_s), lanes0(1, z_s))
+            block = jnp.concatenate([ext[all_rows(j), w] for w in pair], axis=1)
+            rows = pl.ds(0, 2 * BODIES + S * (j + 1))
+            side_term = dot_low(block, jnp.concatenate([ext[rows, w] for w in pair], axis=1))
+            term = dot_low(block, jnp.concatenate([op[:, w] for w in pair], axis=1))
+            width = 2 * BODIES + S * (j + 1)
+            if n > 0:
+                term = term + acc[...]
+                side_term = side_term + side_acc[:, :width]
+            if n < 7:
+                acc[...] = term
+                side_acc[:, :width] = side_term
+        side = side_term[:, BODIES:]
+        side = jnp.concatenate([side_term[:, :BODIES] + side[:, :BODIES], side[:, BODIES:]], axis=1)
+        side_rows = S + 8 * (j // 2)
+        side_out[j, pl.ds(0, S), :] = padded(side) if j < 1 else side[:, :Q]
+        if j == 2:
+            side_out[j, pl.ds(S, 8), :] = jnp.concatenate([side[8 * i : 8 * i + 8, Q:] for i in range(4)], axis=1)
+        out = side_out.at[j, pl.ds(0, side_rows), :]
+        for i in (2, 3, 1):
+            remote(out, sides_in.at[j, c, pl.ds(0, side_rows), :], s_send.at[j], s_recv.at[j], col_peer(i)).start()
+        three = sides_in.at[j, pl.ds(0, 3), pl.ds(0, side_rows), :]
+        pending.append((three, s_send.at[j]))
         for i in range(4):
-            xh_s, z_first = order[i]
-            window = pl.ds(pl.multiple_of((xh_s * 8 + z_first) * 4 * Q, MM_CHUNK), MM_CHUNK)
-            await_chunk(j, xh_s, z_first)
-            term = dot_low(ext[all_rows(j), window], op[:, window])
-            acc = term if acc is None else acc + term
-            term = dot_low(ext[all_rows(j), window], ext[pl.ds(0, BODIES + S * (j + 1)), window])
-            side = term if side is None else side + term
-        for i in range(4):
-            part[j, i] = acc[:, i * Q : (i + 1) * Q]
+            part[j, i] = term[:, i * Q : (i + 1) * Q]
         for i in range(1, 4):
             remote(part.at[j, (c + i) % 4], parts_in.at[j, c], r_send.at[j], r_recv.at[j], col_peer(i)).start()
         pending.append((part.at[j, pl.ds(0, 3)], r_send.at[j]))
         parts_in[j, c] = part[j, c]
-        blocks = 2 if j == 2 else 1
-        side_out[j, 0] = padded(side[:, :Q]) if j < 1 else side[:, :Q]
-        if blocks == 2:
-            side_out[j, 1] = padded(side[:, Q:])
-        out = side_out.at[j, pl.ds(0, blocks)]
-        for i in range(1, 4):
-            remote(out, sides_in.at[j, c, pl.ds(0, blocks)], s_send.at[j], s_recv.at[j], col_peer(i)).start()
-        pending.append((sides_in.at[j, pl.ds(0, 3), pl.ds(0, blocks)], s_send.at[j]))
-        for k in range(blocks):
-            sides_in[j, c, k] = side_out[j, k]
-        await_bytes(sides_in.at[j, pl.ds(0, 3), pl.ds(0, blocks)], s_recv.at[j])
-        sums = [
-            (sides_in[j, 0, k] + sides_in[j, 1, k]) + (sides_in[j, 2, k] + sides_in[j, 3, k]) for k in range(blocks)
-        ]
-        mean = sums[0][:, :BODIES] * (BODIES / N)
-        raw = sums[0][:, BODIES:] * (1.0 / N)
+        sides_in[j, c, pl.ds(0, side_rows), :] = side_out[j, :side_rows, :]
+        await_bytes(three, s_recv.at[j])
+        sums = [sides_in[j, i, :side_rows, :] for i in range(4)]
+        sums = (sums[0] + sums[1]) + (sums[2] + sums[3])
+        sums, extra = sums[:S], sums[S:]
+        mean = sums[:, :BODIES] * (BODIES / N)
+        raw = sums[:, BODIES:] * (1.0 / N)
         if j == 2:
-            raw = jnp.concatenate([raw, sums[1][:, :S] * (1.0 / N)], axis=1)
+            extra = jnp.concatenate([extra[:, S * i : S * i + S] for i in range(4)], axis=0)
+            raw = jnp.concatenate([raw, extra * (1.0 / N)], axis=1)
         gram = raw[:, S * j : S * (j + 1)]
         coef = None
         if j > 0:
@@ -482,15 +485,17 @@
         out_specs=(vmem, vmem, vmem),
         scratch_shapes=[
             pltpu.VMEM((ROWS, COLS), BF16),
-            pltpu.VMEM((BODIES + 3 * S, COLS), BF16),
+            pltpu.VMEM((2 * BODIES + 3 * S, COLS), BF16),
             pltpu.VMEM((BODIES + 4 * S, Q), F32),
             pltpu.VMEM((3 * S, 4 * Q), F32),
             pltpu.VMEM((3, S, Q), BF16),
             pltpu.VMEM((3, 8, H, 2 * Q), BF16),
             pltpu.VMEM((3, 4, S, Q), F32),
             pltpu.VMEM((3, 4, S, Q), F32),
-            pltpu.VMEM((3, 2, S, Q), F32),
-            pltpu.VMEM((3, 4, 2, S, Q), F32),
+            pltpu.VMEM((3, S + 8, Q), F32),
+            pltpu.VMEM((3, 4, S + 8, Q), F32),
+            pltpu.VMEM((S, ROWS), F32),
+            pltpu.VMEM((S, 2 * Q), F32),
             pltpu.VMEM((8, Q), F32),
             pltpu.VMEM((64, 8, Q), F32),
             pltpu.VMEM((S, Q), F32),

time: 118 us -> 112 us (0.949)
  Pallas kernels: 110 us -> 103 us
    pallas_call x1, Pallas kernels: 110 us -> 103 us  [local(): pl.pallas_call(kernel, name='arnoldi', out_shape=(jax.ShapeDtypeStruct((4...]
where the time goes in v3:
time: 112 us; the launch traced here: 111 us
  Pallas kernels  103 us (92%)
  local copies, waits for them, and re-layouts  7.52 us (7%)
    pallas_call x1, Pallas kernels, local(): pl.pallas_call(kernel, name='arnoldi', out_shape=(jax.ShapeDtypeStruct((4...  103 us
    unnamed x10, local copies, waits for them, and re-layouts  6.81 us

profile of v3, /device:TPU:1, one launch (start us, length us, event | category | flops | bytes accessed | tf_op | source)
XLA Modules:
  0.0 111.4 jit_solution(10539353172620214983)
XLA Ops:
  0.6 0.0 copy-start
  0.6 3.4 %copy-done = bf16[512,8192]{1,0:T(8,128)(2,1)S(1)} copy-done((bf16[512,8192]{1,0:T(8,128)(2,1)S(1)}, bf16[512,8192]{1,0:T(8,128)(2,1)}, u32[]{:S(2)}) %copy-start) | copy-done | bytes 8388632
  4.0 0.0 copy-start.1
  4.0 0.8 copy-done.1
  4.9 0.0 copy-start.2
  4.9 0.7 copy-done.2
  5.5 0.0 copy-start.3
  5.5 0.7 copy-done.3
  6.2 103.2 %arnoldi.1 = (f32[128,128]{1,0:T(8,128)S(1)}, f32[128,96]{1,0:T(8,128)S(1)}, f32[32,32]{1,0:T(8,128)S(1)}) custom-call(bf16[512,8192]{1,0:T(8,128)(2,1)S(1)} %copy-done, f32[32,512]{1,0:T(8,128)S(1)} %copy-done.1, s32[1,512]{1,0:T(1,128)S(1)} %bitcast.2, f32[1,512]{1,0:T(1,128)S(1)} %bitcast.3), custom_call_target="tpu_custom_call" | custom-call | tf_op jit(solution)/shard_map/arnoldi/pallas_call | solution.py:476
  109.4 0.7 copy.7
  110.2 0.6 copy.10
  110.8 0.6 copy.11
Async XLA Ops:
  0.6 3.4 %copy-start = (bf16[512,8192]{1,0:T(8,128)(2,1)S(1)}, bf16[512,8192]{1,0:T(8,128)(2,1)}, u32[]{:S(2)}) copy-start(bf16[512,8192]{1,0:T(8,128)(2,1)} %op_hbm.1) | copy-start | bytes 25165828
  4.0 0.8 copy-start.1
  4.9 0.7 copy-start.2
  5.5 0.7 copy-start.3

commit v4 on v3

--- a/solution.py
+++ b/solution.py
@@ -22,6 +22,7 @@
 BF16 = jnp.bfloat16
 OP_CHUNKS = 4
 NEAR = (0, 1, 7, 2, 6, 3, 5, 4)
+FAR = (4, 5, 3, 6, 2, 7, 1, 0)
 
 
 def mm(a, b):
@@ -144,11 +145,8 @@
     barrier = pltpu.get_barrier_semaphore()
 
     def greet(count, peer, first):
-        def body(i, carry):
+        for i in range(first, count):
             pl.semaphore_signal(barrier, inc=1, device_id=peer(i), device_id_type=MESH)
-            return carry
-
-        lax.fori_loop(first, count, body, 0)
         return count - first
 
     root = (y + 4 - c) % 2 == 0
@@ -262,17 +260,21 @@
         at0 = ext.at[top(j), mine]
         sem1, sem_mid, sem0 = g1_recv.at[j, x * 8 + z], gm_recv.at[j, z], g0_recv.at[j, xh * 8 + z]
 
-        def spread1(dst, sem):
-            loop(4, 32, lambda i: remote(src1, dst, g_send.at[j, 1], sem, a1_to(i)).start())
-            loop(1, 4, lambda i: remote(src1, dst, g_send.at[j, 1], sem, a1_to(i)).start())
+        def spread(dst, sem):
+            for d in FAR:
+                for i in (2, 1, 3, 0):
+                    if d or i:
+                        remote(src1, dst, g_send.at[j, 1], sem, a1_to(4 * d + i)).start()
+                for i in (1, 0):
+                    if d or i:
+                        remote(src0, at0, g_send.at[j, 0], sem0, a0_to(2 * d + i)).start()
             either(
                 own1,
                 lambda: pltpu.make_async_copy(src1, dst, sem).start(),
                 lambda: remote(src1, dst, g_send.at[j, 1], sem, a1_to(0)).start(),
             )
 
-        either(straight, lambda: spread1(at1, sem1), lambda: spread1(at_mid, sem_mid))
-        loop(1, 16, lambda i: remote(src0, at0, g_send.at[j, 0], sem0, a0_to(i)).start())
+        either(straight, lambda: spread(at1, sem1), lambda: spread(at_mid, sem_mid))
         either(
             own0,
             lambda: pltpu.make_async_copy(src0, at0, sem0).start(),
@@ -331,7 +333,10 @@
 
     def table_start():
         src, dst = table_out.at[tables, :], table_in.at[here, tables, :]
-        loop(1, 64, lambda i: remote(src, dst, t_sem.at[0], t_sem.at[1], plane_to(i)).start())
+        for d in FAR:
+            for i in range(8 * d, 8 * d + 8):
+                if i:
+                    remote(src, dst, t_sem.at[0], t_sem.at[1], plane_to(i)).start()
         either(
             jnp.logical_and(straight, own1),
             lambda: pltpu.make_async_copy(src, dst, t_sem.at[1]).start(),
@@ -341,14 +346,17 @@
     def table_finish():
         await_bytes(table_in.at[:, tables, :], t_sem.at[1])
 
-        def build(i):
-            plane = jnp.where(ids.astype(F32) == table_in[i, 1:2, :], table_in[i, 0:1, :], 0.0)
-            window = pl.ds(pl.multiple_of(i * Q, Q), Q)
-            high = plane.astype(BF16)
-            ext[pl.ds(0, BODIES), window] = high
-            ext[pl.ds(BODIES, BODIES), window] = (plane - high.astype(F32)).astype(BF16)
-
-        loop(0, 64, build)
+        def build(k):
+            for t in range(4):
+                i = 4 * k + t
+                plane = jnp.where(ids_f == table_in[i, 1:2, :], table_in[i, 0:1, :], 0.0)
+                window = pl.ds(pl.multiple_of(i * Q, Q), Q)
+                high = plane.astype(BF16)
+                ext[pl.ds(0, BODIES), window] = high
+                ext[pl.ds(BODIES, BODIES), window] = (plane - high.astype(F32)).astype(BF16)
+
+        ids_f = ids.astype(F32)
+        loop(0, 16, build)
 
     def padded(value):
         return jnp.concatenate([value, jnp.zeros((S, Q - value.shape[1]), F32)], axis=1)

time: 112 us -> 109 us (0.973)
  Pallas kernels: 103 us -> 101 us
    pallas_call x1, Pallas kernels: 103 us -> 101 us  [local(): pl.pallas_call(kernel, name='arnoldi', out_shape=(jax.ShapeDtypeStruct((4...]
where the time goes in v4:
time: 109 us
  Pallas kernels  101 us (93%)
  local copies, waits for them, and re-layouts  7.52 us (7%)
    pallas_call x1, Pallas kernels, local(): pl.pallas_call(kernel, name='arnoldi', out_shape=(jax.ShapeDtypeStruct((4...  101 us
    unnamed x10, local copies, waits for them, and re-layouts  6.81 us

profile of v4, /device:TPU:1, one launch (start us, length us, event | category | flops | bytes accessed | tf_op | source)
XLA Modules:
  0.0 108.7 jit_solution(11267160324819710312)
XLA Ops:
  0.6 0.0 copy-start
  0.6 3.4 %copy-done = bf16[512,8192]{1,0:T(8,128)(2,1)S(1)} copy-done((bf16[512,8192]{1,0:T(8,128)(2,1)S(1)}, bf16[512,8192]{1,0:T(8,128)(2,1)}, u32[]{:S(2)}) %copy-start) | copy-done | bytes 8388632
  4.0 0.0 copy-start.1
  4.0 0.8 copy-done.1
  4.9 0.0 copy-start.2
  4.9 0.7 copy-done.2
  5.5 0.0 copy-start.3
  5.5 0.7 copy-done.3
  6.2 100.5 %arnoldi.1 = (f32[128,128]{1,0:T(8,128)S(1)}, f32[128,96]{1,0:T(8,128)S(1)}, f32[32,32]{1,0:T(8,128)S(1)}) custom-call(bf16[512,8192]{1,0:T(8,128)(2,1)S(1)} %copy-done, f32[32,512]{1,0:T(8,128)S(1)} %copy-done.1, s32[1,512]{1,0:T(1,128)S(1)} %bitcast.2, f32[1,512]{1,0:T(1,128)S(1)} %bitcast.3), custom_call_target="tpu_custom_call" | custom-call | tf_op jit(solution)/shard_map/arnoldi/pallas_call | solution.py:484
  106.8 0.7 copy.7
  107.5 0.6 copy.10
  108.1 0.6 copy.11
Async XLA Ops:
  0.6 3.4 %copy-start = (bf16[512,8192]{1,0:T(8,128)(2,1)S(1)}, bf16[512,8192]{1,0:T(8,128)(2,1)}, u32[]{:S(2)}) copy-start(bf16[512,8192]{1,0:T(8,128)(2,1)} %op_hbm.1) | copy-start | bytes 25165828
  4.0 0.8 copy-start.1
  4.9 0.7 copy-start.2
  5.5 0.7 copy-start.3

commit v5 on v4

--- a/solution.py
+++ b/solution.py
@@ -46,10 +46,16 @@
     lane_id = lax.broadcasted_iota(jnp.int32, (S, Q), 1)
     eye = (lane_id == row_id + S).astype(F32)
     work = jnp.concatenate([gram, jnp.zeros((S, Q - S), F32)], axis=1) + eye
-    for k in range(S - 1):
-        col = jnp.broadcast_to(work[:, k : k + 1], (S, Q))
-        share = jnp.where(row_id > k, col * work[k : k + 1, :], 0.0)
-        work = work - share * (1.0 / col[k : k + 1, :])
+    for k in range(0, S, 2):
+        a = jnp.broadcast_to(work[:, k : k + 1], (S, Q))
+        b = jnp.broadcast_to(work[:, k + 1 : k + 2], (S, Q))
+        first, second = work[k : k + 1, :], work[k + 1 : k + 2, :]
+        scale = 1.0 / a[k : k + 1, :]
+        first = first * scale
+        second = second - a[k + 1 : k + 2, :] * first
+        b = b - a * (b[k : k + 1, :] * scale)
+        rest = work - a * first - b * (second * (1.0 / b[k + 1 : k + 2, :]))
+        work = jnp.where(row_id > k + 1, rest, jnp.where(row_id == k + 1, second, work))
     pivots = jnp.sum(jnp.where(lane_id == row_id, work, 0.0), axis=1, keepdims=True)
     r = lax.rsqrt(pivots)
     work = work * (r * (1.5 - 0.5 * pivots * r * r))

time: 109 us -> 105 us (0.963)
  Pallas kernels: 101 us -> 96.8 us
    pallas_call x1, Pallas kernels: 101 us -> 96.8 us  [local(): pl.pallas_call(kernel, name='arnoldi', out_shape=(jax.ShapeDtypeStruct((4...]
where the time goes in v5:
time: 105 us
  Pallas kernels  96.8 us (92%)
  local copies, waits for them, and re-layouts  7.52 us (7%)
    pallas_call x1, Pallas kernels, local(): pl.pallas_call(kernel, name='arnoldi', out_shape=(jax.ShapeDtypeStruct((4...  96.8 us
    unnamed x10, local copies, waits for them, and re-layouts  6.81 us

profile of v5, /device:TPU:1, one launch (start us, length us, event | category | flops | bytes accessed | tf_op | source)
XLA Modules:
  0.0 104.9 jit_solution(2276594164498693606)
XLA Ops:
  0.6 0.0 copy-start
  0.6 3.4 %copy-done = bf16[512,8192]{1,0:T(8,128)(2,1)S(1)} copy-done((bf16[512,8192]{1,0:T(8,128)(2,1)S(1)}, bf16[512,8192]{1,0:T(8,128)(2,1)}, u32[]{:S(2)}) %copy-start) | copy-done | bytes 8388632
  4.0 0.0 copy-start.1
  4.0 0.8 copy-done.1
  4.9 0.0 copy-start.2
  4.9 0.7 copy-done.2
  5.5 0.0 copy-start.3
  5.5 0.7 copy-done.3
  6.2 96.8 %arnoldi.1 = (f32[128,128]{1,0:T(8,128)S(1)}, f32[128,96]{1,0:T(8,128)S(1)}, f32[32,32]{1,0:T(8,128)S(1)}) custom-call(bf16[512,8192]{1,0:T(8,128)(2,1)S(1)} %copy-done, f32[32,512]{1,0:T(8,128)S(1)} %copy-done.1, s32[1,512]{1,0:T(1,128)S(1)} %bitcast.2, f32[1,512]{1,0:T(1,128)S(1)} %bitcast.3), custom_call_target="tpu_custom_call" | custom-call | tf_op jit(solution)/shard_map/arnoldi/pallas_call | solution.py:490
  103.0 0.7 copy.7
  103.7 0.6 copy.10
  104.3 0.6 copy.11
Async XLA Ops:
  0.6 3.4 %copy-start = (bf16[512,8192]{1,0:T(8,128)(2,1)S(1)}, bf16[512,8192]{1,0:T(8,128)(2,1)}, u32[]{:S(2)}) copy-start(bf16[512,8192]{1,0:T(8,128)(2,1)} %op_hbm.1) | copy-start | bytes 25165828
  4.0 0.8 copy-start.1
  4.9 0.7 copy-start.2
  5.5 0.7 copy-start.3
